TPU v7x, 32 devices: a whole 2x2x4 slice. The times are simulated.
32 devices in a mesh: orient: 16 (over z, y, core), frame: 2 (over x).
Axes of the slice: x: 2, y: 2, z: 4, core: 2. Of those that a mesh axis runs over, the one named last changes fastest.
Arguments:
- log_tomograms: bfloat16 [2048, 4096], P('orient'), may hold values from -3 to 3
- frames: int32 [512, 4096], P('frame'), may hold values from 0 to 15, as said below
- tile_index: int32 [2, 32, 2048], P(None, 'frame', 'orient'), may hold values from 0 to 383
- tile_weight: float32 [2, 32, 2048], P(None, 'frame', 'orient'), may hold values from 0.1 to 1
- prior_volume: float32 [2, 384, 128], P('frame', 'orient'), may hold values from 0.5 to 2
Outputs:
- new_log_tomograms: bfloat16 [2048, 4096], P('orient', 'frame')
- volume: float32 [2, 384, 128], P('frame', 'orient')
- evidence: float32 [512], P('frame')
Inputs may be any that keep to these rules, and one draw needn't show every extreme that they name: `frames`: each frame's counts lie below a level of that frame; the first frame has a pixel with 15 photons. `tile_index`: the tile of an entry counts within the shell group of its pixel block.
All inputs are finite; a program needn't handle non-finite values.
Results may differ from a plain program's by a relative error of at most 0.008.
Values may be sent and summed in bfloat16 or wider, within the bound.
A program may use at most 64 MiB of HBM per device.

v0:
```python
import functools

import jax
import jax.numpy as jnp
from jax import lax
from jax.experimental import pallas as pl
from jax.experimental.pallas import tpu as pltpu
from jax.sharding import PartitionSpec as P

MESH = pl.DeviceIdType.MESH
F32 = jnp.float32
BF16 = jnp.bfloat16
PARTS = 4


def remote(src, dst, send_sem, recv_sem, where):
    return pltpu.make_async_remote_copy(
        src_ref=src,
        dst_ref=dst,
        send_sem=send_sem,
        recv_sem=recv_sem,
        device_id=where,
        device_id_type=MESH,
    )


def kernel(
    n_orient,
    n_frame,
    logt_hbm,
    frames_hbm,
    index_hbm,
    weight_hbm,
    prior_hbm,
    new_log_ref,
    volume_ref,
    evidence_ref,
    logt,
    frames,
    index_ref,
    weight_ref,
    prior_ref,
    counts,
    other,
    intensity,
    scores,
    stat_mine,
    stat_in,
    resp_out,
    resp_in,
    den_out,
    den_in,
    numer,
    spread,
    update,
    sums,
    tile_out,
    tile_in,
    tiles,
    tiles_t,
    in_sem,
    count_send,
    count_recv,
    relay_send,
    relay_recv,
    resp_send,
    resp_recv,
    den_send,
    den_recv,
    fan_send,
    fan_recv,
):
    me = lax.axis_index("orient")
    mine = lax.axis_index("frame")
    rot_rows, pixels = logt.shape
    frame_rows = frames.shape[0]
    group_blocks = index_ref.shape[1]
    tile_rows, width = prior_ref.shape[1:]
    columns = pixels // n_frame
    tile_count = tile_rows * n_orient
    chunk = (384 // tile_rows if n_orient % max(384 // tile_rows, 1) == 0 else 1) * tile_rows
    partner = me + 1 - 2 * lax.rem(me, 2)
    across = me + 2 - 4 * lax.rem(me // 2, 2)
    fourth = frame_rows // 4
    part = fourth // PARTS

    logt_copy = pltpu.make_async_copy(logt_hbm, logt, in_sem.at[0])
    logt_copy.start()
    step = frame_rows // PARTS
    frame_copies = []
    for c in range(PARTS):
        rows = pl.ds(c * step, step)
        copy = pltpu.make_async_copy(frames_hbm.at[rows], frames.at[rows], in_sem.at[1 + c])
        copy.start()
        frame_copies.append(copy)

    small_copies = []
    for i, (source, target) in enumerate(
        ((index_hbm, index_ref), (weight_hbm, weight_ref), (prior_hbm, prior_ref))
    ):
        copy = pltpu.make_async_copy(source, target, in_sem.at[1 + PARTS + i])
        copy.start()
        small_copies.append(copy)

    barrier = pltpu.get_barrier_semaphore()

    def greet(d, carry):
        pl.semaphore_signal(
            barrier, inc=1, device_id={"orient": lax.rem(me + d, n_orient)}, device_id_type=MESH
        )
        return carry

    lax.fori_loop(1, n_orient, greet, 0)
    for d in range(1, n_frame):
        pl.semaphore_signal(
            barrier, inc=1, device_id={"frame": lax.rem(mine + d, n_frame)}, device_id_type=MESH
        )

    for c in range(PARTS):
        frame_copies[c].wait()
        counts[c * step : (c + 1) * step] = (
            frames[c * step : (c + 1) * step].astype(F32).astype(BF16)
        )
    logt_copy.wait()
    mass = jnp.zeros((rot_rows, 128), F32)
    for c in range(pixels // 512):
        value = jnp.exp(logt[:, c * 512 : (c + 1) * 512].astype(F32))
        intensity[:, c * 512 : (c + 1) * 512] = value
        for k in range(4):
            mass = mass + value[:, k * 128 : (k + 1) * 128]
    mass = jnp.sum(mass, axis=1, keepdims=True)
    correlation = lax.dot_general(
        logt[...], counts[...], (((1,), (1,)), ((), ())), preferred_element_type=F32
    )
    score = (64.0 / pixels) * (correlation - mass)
    scores[...] = score
    peak = jnp.max(score, axis=0, keepdims=True)
    stat_mine[0:1, :] = peak
    stat_mine[1:2, :] = jnp.sum(jnp.exp(score - peak), axis=0, keepdims=True)

    pl.semaphore_wait(barrier, n_orient - 1 + n_frame - 1)

    def quarter(owner, c):
        return pl.ds(pl.multiple_of(lax.rem(owner, 4) * fourth + c * part, 16), part)

    count_copies = []
    for c in range(PARTS):
        for d in range(1, n_frame):
            to = lax.rem(mine + d, n_frame)
            copy = remote(
                counts.at[quarter(me, c), pl.ds(pl.multiple_of(to * columns, 128), columns)],
                other.at[d - 1, quarter(me, c)],
                count_send.at[d - 1, c],
                count_recv.at[d - 1, c],
                {"frame": to},
            )
            copy.start()
            count_copies.append((d, c, copy))

    def send_stat(d, carry):
        remote(
            stat_mine,
            stat_in.at[d - 1],
            fan_send.at[0],
            fan_recv.at[0],
            {"orient": lax.rem(me + d, n_orient)},
        ).start()
        return carry

    lax.fori_loop(1, n_orient, send_stat, 0)

    for copy in small_copies:
        copy.wait()

    weight_low = weight_ref[...].astype(BF16).astype(F32)
    index = index_ref[...]
    lane = lax.broadcasted_iota(jnp.int32, (8, 128), 1)
    joint = spread.shape[1] // tile_rows
    strip = joint * tile_rows

    def build(o, carry):
        first = o * strip
        row_id = lax.broadcasted_iota(jnp.int32, (strip, rot_rows), 0) + first
        total = jnp.zeros((strip, rot_rows), F32)
        for j in range(group_blocks):
            value = jnp.where(row_id == index[0, j][None, :], weight_low[0, j][None, :], 0.0)
            value = value + jnp.where(
                row_id == index[1, j][None, :], weight_low[1, j][None, :], 0.0
            )
            low = value.astype(BF16)
            total = total + low.astype(F32)
            spread[o, :, j * rot_rows : (j + 1) * rot_rows] = low
        weight_sum = jnp.sum(total, axis=1, keepdims=True)
        for i in range(joint):
            packed = jnp.zeros((8, 128), F32)
            for b in range(tile_rows // 8):
                at = i * tile_rows + b * 8
                exact = weight_sum[at : at + 8]
                high = exact.astype(BF16).astype(F32)
                packed = packed + jnp.where(lane == b, high, 0.0)
                packed = packed + jnp.where(lane == 64 + b, exact - high, 0.0)
            sums[o * joint + i] = packed
        return carry

    lax.fori_loop(0, n_orient // joint, build, 0)

    relay_copies = []

    def relay(owner, d, c, kind, to):
        where = other.at[d - 1, quarter(owner, c)]
        copy = remote(
            where,
            where,
            relay_send.at[kind, d - 1, c],
            relay_recv.at[kind, d - 1, c],
            {"orient": to},
        )
        copy.start()
        relay_copies.append((kind, d, c, copy))

    def relay_first(start, stop):
        for d, c, copy in count_copies:
            if start <= c < stop:
                copy.wait_recv()
                relay(me, d, c, 0, across)
                relay(me, d, c, 1, partner)

    def relay_second(start, stop):
        for kind, d, c, copy in list(relay_copies):
            if kind == 0 and start <= c < stop:
                copy.wait_recv()
                relay(across, d, c, 2, partner)

    relay_first(0, 2)

    fan_wait_recv = pltpu.make_async_copy(stat_in, stat_in, fan_recv.at[0])
    fan_wait_send = pltpu.make_async_copy(stat_in, stat_in, fan_send.at[0])
    fan_wait_recv.wait()
    peaks = stat_in[:, 0, :]
    totals = stat_in[:, 1, :]
    peak_mine = stat_mine[0:1, :]
    peak = jnp.maximum(jnp.max(peaks, axis=0, keepdims=True), peak_mine)
    total = stat_mine[1:2, :] * jnp.exp(peak_mine - peak) + jnp.sum(
        totals * jnp.exp(peaks - peak), axis=0, keepdims=True
    )
    evidence_ref[...] = peak + jnp.log(total)
    resp = jnp.exp(scores[...] - peak) / total
    resp_out[...] = resp.astype(BF16)
    den = jnp.sum(resp, axis=1, keepdims=True).astype(BF16)
    den_out[...] = jnp.broadcast_to(den, (rot_rows, 128))

    resp_copies = []
    for d in range(1, n_frame):
        to = {"frame": lax.rem(mine + d, n_frame)}
        copy = remote(resp_out, resp_in.at[d - 1], resp_send.at[d - 1], resp_recv.at[d - 1], to)
        copy.start()
        den_copy = remote(den_out, den_in.at[d - 1], den_send.at[d - 1], den_recv.at[d - 1], to)
        den_copy.start()
        resp_copies.append((copy, den_copy))
    fan_wait_send.wait()

    span = min(columns, 512)
    first = pl.multiple_of(mine * columns, 128)
    for c in range(columns // span):
        mixed = jnp.dot(
            resp_out[...],
            counts[:, pl.ds(pl.multiple_of(first + c * span, 128), span)],
            preferred_element_type=F32,
        )
        numer[:, c * span : (c + 1) * span] = mixed.astype(BF16).astype(F32)

    relay_first(2, PARTS)
    relay_second(0, PARTS)
    for copy, den_copy in resp_copies:
        copy.wait_recv()
        den_copy.wait_recv()
    for kind, d, c, copy in relay_copies:
        if kind > 0:
            copy.wait_recv()

    share = frame_rows * n_frame / (rot_rows * n_orient)
    den_all = den_out[...].astype(F32)
    for d in range(1, n_frame):
        den_all = den_all + den_in[d - 1].astype(F32)
    inverse = 1.0 / (den_all + share)
    for c in range(columns // span):
        cols = slice(c * span, (c + 1) * span)
        value = numer[:, cols]
        for d in range(1, n_frame):
            mixed = jnp.dot(resp_in[d - 1], other[d - 1, :, cols], preferred_element_type=F32)
            value = value + mixed.astype(BF16).astype(F32)
        value = value + share * intensity[:, pl.ds(pl.multiple_of(first + c * span, 128), span)]
        for k in range(span // width):
            j = c * (span // width) + k
            new = value[:, k * width : (k + 1) * width] * inverse
            high = new.astype(BF16)
            update[j * rot_rows : (j + 1) * rot_rows, 0:width] = high
            update[j * rot_rows : (j + 1) * rot_rows, width : 2 * width] = (
                new - high.astype(F32)
            ).astype(BF16)

    owners = chunk // tile_rows

    def gather_in(c, carry):
        block = spread[pl.ds(c * (chunk // strip), chunk // strip)].reshape(chunk, group_blocks * rot_rows)
        summed = jnp.dot(block, update[...], preferred_element_type=F32)
        summed = summed[:, 0:width] + summed[:, width : 2 * width]
        for i in range(owners):
            own = summed[i * tile_rows : (i + 1) * tile_rows]
            message = jnp.concatenate([own, sums[c * owners + i]], axis=0)
            tile_out[c * owners + i] = message.astype(BF16)
        return carry

    lax.fori_loop(0, tile_count // chunk, gather_in, 0)

    def send_tiles(d, carry):
        to = lax.rem(me + d, n_orient)
        remote(
            tile_out.at[to], tile_in.at[d - 1], fan_send.at[1], fan_recv.at[1], {"orient": to}
        ).start()
        return carry

    lax.fori_loop(1, n_orient, send_tiles, 0)
    pltpu.make_async_copy(tile_in, tile_in, fan_recv.at[1]).wait()
    whole = lax.fori_loop(0, n_orient - 1, lambda d, so_far: so_far + tile_in[d].astype(F32), tile_out[me].astype(F32))
    prior_weight = rot_rows * group_blocks / (4.0 * tile_rows)
    weight = [
        whole[tile_rows:, b : b + 1] + whole[tile_rows:, 64 + b : 65 + b]
        for b in range(tile_rows // 8)
    ]
    weight = jnp.concatenate(weight, axis=0)
    value = whole[0:tile_rows] + prior_weight * prior_ref[0]
    value = value / (weight + prior_weight)
    volume_ref[0] = value
    tiles[me] = (value - 1.0).astype(BF16)

    def send_volume(d, carry):
        own = tiles.at[me]
        remote(
            own, own, fan_send.at[2], fan_recv.at[2], {"orient": lax.rem(me + d, n_orient)}
        ).start()
        return carry

    lax.fori_loop(1, n_orient, send_volume, 0)
    for d, c, copy in count_copies:
        copy.wait_send()
    for kind, d, c, copy in relay_copies:
        copy.wait_send()
    for copy, den_copy in resp_copies:
        copy.wait_send()
        den_copy.wait_send()
    pltpu.make_async_copy(tile_in, tile_in, fan_send.at[1]).wait()
    incoming = tiles.at[pl.ds(0, n_orient - 1)]
    pltpu.make_async_copy(incoming, incoming, fan_recv.at[2]).wait()

    def turn(c, carry):
        value = tiles[pl.ds(c * owners, owners)].astype(F32).reshape(chunk, width)
        tiles_t[:, pl.ds(pl.multiple_of(c * chunk, 128), chunk)] = value.T.astype(BF16)
        return carry

    lax.fori_loop(0, tile_count // chunk, turn, 0)
    both = weight_low[0] + weight_low[1]
    both = jnp.where(index[0] == index[1], both.astype(BF16).astype(F32), both)
    scale = 1.0 / both
    pair = 2 if group_blocks % 2 == 0 else 1
    for c in range(group_blocks // pair):
        cols = slice(c * pair * rot_rows, (c + 1) * pair * rot_rows)
        block = spread[:, :, cols].reshape(tile_count, pair * rot_rows)
        blended = jnp.dot(tiles_t[...], block, preferred_element_type=F32)
        for k in range(pair):
            j = c * pair + k
            value = blended[:, k * rot_rows : (k + 1) * rot_rows] * scale[j][None, :]
            value = jnp.log(1.0 + value)
            new_log_ref[:, j * width : (j + 1) * width] = value.T.astype(BF16)
    pltpu.make_async_copy(incoming, incoming, fan_send.at[2]).wait()


def place(a_in, b_in, c_in, a_out, b_out, c_out, sem):
    copies = [
        pltpu.make_async_copy(source, target, sem.at[i])
        for i, (source, target) in enumerate(((a_in, a_out), (b_in, b_out), (c_in, c_out)))
    ]
    for copy in copies:
        copy.start()
    for copy in copies:
        copy.wait()


def on_device(log_tomograms, frames, tile_index, tile_weight, prior_volume):
    n_orient = lax.axis_size("orient")
    n_frame = lax.axis_size("frame")
    rot_rows, pixels = log_tomograms.shape
    frame_rows = frames.shape[0]
    group_blocks = tile_index.shape[1]
    tile_rows, width = prior_volume.shape[1:]
    columns = pixels // n_frame
    tile_count = tile_rows * n_orient
    others = max(n_frame - 1, 1)
    dma = pltpu.SemaphoreType.DMA
    vmem = pl.BlockSpec(memory_space=pltpu.VMEM)
    hbm = pl.BlockSpec(memory_space=pltpu.HBM)
    new_log, volume, evidence = pl.pallas_call(
        functools.partial(kernel, n_orient, n_frame),
        out_shape=(
            pltpu.VMEM((rot_rows, columns), BF16),
            pltpu.VMEM((1, tile_rows, width), F32),
            pltpu.VMEM((1, frame_rows), F32),
        ),
        in_specs=[hbm] * 5,
        out_specs=(vmem, vmem, vmem),
        scratch_shapes=[
            pltpu.VMEM((rot_rows, pixels), BF16),
            pltpu.VMEM((frame_rows, pixels), jnp.int32),
            pltpu.VMEM(tile_index.shape, jnp.int32),
            pltpu.VMEM(tile_weight.shape, F32),
            pltpu.VMEM(prior_volume.shape, F32),
            pltpu.VMEM((frame_rows, pixels), BF16),
            pltpu.VMEM((others, frame_rows, columns), BF16),
            pltpu.VMEM((rot_rows, pixels), F32),
            pltpu.VMEM((rot_rows, frame_rows), F32),
            pltpu.VMEM((2, frame_rows), F32),
            pltpu.VMEM((n_orient - 1, 2, frame_rows), F32),
            pltpu.VMEM((rot_rows, frame_rows), BF16),
            pltpu.VMEM((others, rot_rows, frame_rows), BF16),
            pltpu.VMEM((rot_rows, 128), BF16),
            pltpu.VMEM((others, rot_rows, 128), BF16),
            pltpu.VMEM((rot_rows, columns), F32),
            pltpu.VMEM((n_orient // 2, 2 * tile_rows, group_blocks * rot_rows), BF16),
            pltpu.VMEM((group_blocks * rot_rows, 2 * width), BF16),
            pltpu.VMEM((n_orient, 8, width), F32),
            pltpu.VMEM((n_orient, tile_rows + 8, width), BF16),
            pltpu.VMEM((n_orient - 1, tile_rows + 8, width), BF16),
            pltpu.VMEM((n_orient, tile_rows, width), BF16),
            pltpu.VMEM((width, tile_count), BF16),
            dma((4 + PARTS,)),
            dma((others, PARTS)),
            dma((others, PARTS)),
            dma((3, others, PARTS)),
            dma((3, others, PARTS)),
            dma((others,)),
            dma((others,)),
            dma((others,)),
            dma((others,)),
            dma((3,)),
            dma((3,)),
        ],
        compiler_params=pltpu.CompilerParams(
            collective_id=0, has_side_effects=True, vmem_limit_bytes=48 * 1024 * 1024
        ),
    )(*(
        pltpu.with_memory_space_constraint(value, pltpu.HBM)
        for value in (log_tomograms, frames, tile_index, tile_weight, prior_volume)
    ))
    made = (new_log, volume, evidence)
    new_log, volume, evidence = pl.pallas_call(
        place,
        out_shape=tuple(jax.ShapeDtypeStruct(value.shape, value.dtype) for value in made),
        in_specs=[vmem] * 3,
        out_specs=(hbm,) * 3,
        scratch_shapes=[dma((3,))],
        compiler_params=pltpu.CompilerParams(vmem_limit_bytes=4 * 1024 * 1024),
    )(*made)
    return (new_log, volume, evidence.reshape(frame_rows))


def solution(mesh):
    placed = (
        P("orient", None),
        P("frame", None),
        P(None, "frame", "orient"),
        P(None, "frame", "orient"),
        P("frame", "orient", None),
    )
    return jax.shard_map(
        on_device,
        mesh=mesh,
        in_specs=placed,
        out_specs=(P("orient", "frame"), P("frame", "orient", None), P("frame")),
        check_vma=False,
    )
```

profile of v0, /device:TPU:0, one launch (start us, length us, event | category | flops | bytes accessed | tf_op | source)
XLA Modules:
  0.0 33.0 jit_solution(11205624788964185018)
XLA Ops:
  0.6 31.5 %shard_map.76 = (bf16[128,2048]{1,0:T(8,128)(2,1)S(1)}, f32[1,24,128]{2,1,0:T(8,128)S(1)}, f32[1,256]{1,0:T(1,128)S(1)}) custom-call(bf16[128,4096]{1,0:T(8,128)(2,1)} %logt_hbm.1, s32[256,4096]{1,0:T(8,128)} %frames_hbm.1, s32[2,16,128]{2,1,0:T(8,128)} %index_hbm.1, f32[2,16,128]{2,1,0:T(8,128)} %weight_hbm.1, f32[1,24,128]{2,1,0:T(8,128)} %prior_hbm.1), custom_call_target="tpu_custom_call" | custom-call | tf_op jit(solution)/shard_map/pallas_call | solution.py:402
  32.2 0.8 %shard_map.77 = (bf16[128,2048]{1,0:T(8,128)(2,1)}, f32[1,24,128]{2,1,0:T(8,128)}, f32[1,256]{1,0:T(1,128)}) custom-call(bf16[128,2048]{1,0:T(8,128)(2,1)S(1)} %get-tuple-element.9.a_in, f32[1,24,128]{2,1,0:T(8,128)S(1)} %get-tuple-element.10.b_in, f32[1,256]{1,0:T(1,128)S(1)} %get-tuple-element.11.c_in), custom_call_target="tpu_custom_call" | custom-call | tf_op jit(solution)/shard_map/pallas_call | solution.py:455
where the time goes:
time: 33.2 us; the launch traced here: 33 us
  Pallas kernels  32.4 us (98%)
  between operations  0.64 us (2%)
    pallas_call x1, Pallas kernels, on_device(): pl.pallas_call(functools.partial(kernel, n_orient, n_frame), out_shape=(p...  31.5 us
    pallas_call x1, Pallas kernels, on_device(): pl.pallas_call(place, out_shape=tuple((jax.ShapeDtypeStruct(value.shape,...  0.83 us

commit v1 on v0

v1 whole, which is shorter than its diff:
```python
import functools

import jax
import jax.numpy as jnp
from jax import lax
from jax.experimental import pallas as pl
from jax.experimental.pallas import tpu as pltpu
from jax.sharding import PartitionSpec as P

MESH = pl.DeviceIdType.MESH
F32 = jnp.float32
BF16 = jnp.bfloat16
GROUP = 8
CHUNKS = 4
OWN = 2


def remote(src, dst, send_sem, recv_sem, where):
    return pltpu.make_async_remote_copy(
        src_ref=src,
        dst_ref=dst,
        send_sem=send_sem,
        recv_sem=recv_sem,
        device_id=where,
        device_id_type=MESH,
    )


def far_first(count):
    return sorted(range(1, count), key=lambda d: -min(d, count - d))


def each(order, body):
    if len(order) <= 32:
        for d in order:
            body(d)
    else:

        def step(d, carry):
            body(d)
            return carry

        lax.fori_loop(1, len(order) + 1, step, 0)


def kernel(
    n_orient,
    n_frame,
    logt_hbm,
    frames_hbm,
    index_hbm,
    weight_hbm,
    prior_hbm,
    new_log_ref,
    volume_ref,
    evidence_ref,
    logt,
    frames,
    index_ref,
    weight_ref,
    prior_ref,
    away,
    pool,
    intensity,
    share_all,
    stat_all,
    resp_all,
    spread,
    update,
    sums,
    sums_in,
    gathered,
    tile_out,
    tile_in,
    tiles,
    tiles_t,
    in_sem,
    hello,
    count_send,
    count_recv,
    share_send,
    share_recv,
    fan_send,
    fan_recv,
):
    me = lax.axis_index("orient")
    mine = lax.axis_index("frame")
    rot_rows = logt.shape[1]
    frame_rows = frames.shape[1]
    group_blocks = index_ref.shape[1]
    tile_rows, width = prior_ref.shape[1:]
    columns = logt.shape[2]
    pixels = columns * n_frame
    tile_count = tile_rows * n_orient
    chunk = (384 // tile_rows if n_orient % max(384 // tile_rows, 1) == 0 else 1) * tile_rows
    piece = frame_rows // GROUP
    hop = columns // CHUNKS

    place_in = lax.rem(me, GROUP)
    base = me - place_in
    core = lax.rem(place_in, 2)
    low = lax.rem(place_in // 2, 2)
    high = place_in // 4
    parity = lax.rem(low + high, 2)
    partner = me + 1 - 2 * core
    beside = me + 2 - 4 * low
    above = me + 4 - 8 * high

    barrier = pltpu.get_barrier_semaphore()

    def signal(sem, where):
        pl.semaphore_signal(sem, inc=1, device_id=where, device_id_type=MESH)

    groups = n_orient // GROUP

    def greet_group(sem):
        for i in range(1, GROUP):
            signal(sem, {"orient": base + lax.rem(place_in + i, GROUP)})

    def greet_frames(sem):
        for d in range(1, n_frame):
            signal(sem, {"frame": lax.rem(mine + d, n_frame)})

    greet_frames(barrier)
    greet_group(barrier)
    each(
        list(range(1, groups)),
        lambda k: signal(barrier, {"orient": lax.rem(me + k * GROUP, n_orient)}),
    )

    def rows_of(quarter):
        return pl.ds(pl.multiple_of(quarter * 2 * piece, 2 * piece), 2 * piece)

    def columns_of(d):
        return pl.ds(pl.multiple_of(lax.rem(mine + d, n_frame) * columns, 128), columns)

    my_quarter = parity * 2 + core

    def load(source, target, sem):
        copy = pltpu.make_async_copy(source, target, sem)
        copy.start()
        return copy

    first_copies = [
        load(
            frames_hbm.at[rows_of(my_quarter), columns_of(d)],
            frames.at[d, rows_of(my_quarter)],
            in_sem.at[0, d],
        )
        for d in range(1, n_frame)
    ]
    logt_copies = {}
    rest_copies = {}
    for d in range(1, n_frame):
        logt_copies[d] = load(logt_hbm.at[:, columns_of(d)], logt.at[d], in_sem.at[1, d])
        for i in range(1, 4):
            rows = rows_of(lax.rem(my_quarter + i, 4))
            load(frames_hbm.at[rows, columns_of(d)], frames.at[d, rows], in_sem.at[2, d])
        rest = frames.at[d, pl.ds(0, 6 * piece)]
        rest_copies[d] = pltpu.make_async_copy(rest, rest, in_sem.at[2, d])
    logt_copies[0] = load(logt_hbm.at[:, columns_of(0)], logt.at[0], in_sem.at[0, 0])
    own_copies = []
    own = columns // OWN
    for c in range(OWN):
        cols = pl.ds(pl.multiple_of(mine * columns + c * own, 128), own)
        own_copies.append(
            load(
                frames_hbm.at[:, cols],
                frames.at[0, :, pl.ds(c * own, own)],
                in_sem.at[1 + c, 0],
            )
        )
    small_copies = [
        load(source, target, in_sem.at[3, i])
        for i, (source, target) in enumerate(((index_hbm, index_ref), (weight_hbm, weight_ref)))
    ]
    small_copies.append(load(prior_hbm, prior_ref, in_sem.at[4, 0]))

    for d in range(1, n_frame):
        first_copies[d - 1].wait()
        away[d - 1, rows_of(my_quarter)] = frames[d, rows_of(my_quarter)].astype(F32).astype(BF16)

    pl.semaphore_wait(barrier, GROUP - 1 + groups - 1 + n_frame - 1)

    def part_rows(side, kind):
        return pl.ds(
            pl.multiple_of((side * 4 + core * 2 + kind) * piece, piece), piece
        )

    def part_cols(k, start=0):
        return pl.ds(pl.multiple_of(start + k * hop, 128), hop)

    def source_of(d):
        return lax.rem(mine + n_frame - d, n_frame)

    relayed = part_rows(parity, low)
    kept = part_rows(parity, 1 - low)
    cross = {}
    for kind, rows in ((0, relayed), (1, kept)):
        for k in range(CHUNKS):
            for d in range(1, n_frame):
                cross[kind, k, d] = remote(
                    away.at[d - 1, rows, part_cols(k)],
                    pool.at[mine, rows, part_cols(k)],
                    count_send.at[0],
                    count_recv.at[kind, d - 1, k],
                    {"frame": lax.rem(mine + d, n_frame)},
                )
                cross[kind, k, d].start()
    greet_group(hello.at[0])

    onward = {}

    def send_on(kind, rows, k, d, to):
        where = pool.at[source_of(d), rows, part_cols(k)]
        onward[kind, k, d] = remote(
            where, where, count_send.at[0], count_recv.at[kind, d - 1, k], {"orient": to}
        )
        onward[kind, k, d].start()

    def relay(k):
        for d in range(1, n_frame):
            cross[0, k, d].wait_recv()
            send_on(2, relayed, k, d, beside)
            send_on(3, relayed, k, d, above)

    def pass_on(k):
        for d in range(1, n_frame):
            onward[2, k, d].wait_recv()
            onward[3, k, d].wait_recv()
            send_on(4, rows_of((1 - parity) * 2 + core), k, d, partner)
        for d in range(1, n_frame):
            cross[1, k, d].wait_recv()
            send_on(5, rows_of(my_quarter), k, d, partner)

    def arrived(k):
        for d in range(1, n_frame):
            onward[4, k, d].wait_recv()
            onward[5, k, d].wait_recv()

    mass = jnp.zeros((rot_rows, 128), F32)
    correlation = jnp.zeros((rot_rows, frame_rows), F32)
    contract = (((1,), (1,)), ((), ()))

    def exponentials(slot, mass):
        for c in range(columns // 512 if columns % 512 == 0 else 1):
            span = min(columns, 512)
            value = jnp.exp(logt[slot, :, c * span : (c + 1) * span].astype(F32))
            if slot == 0:
                intensity[:, c * span : (c + 1) * span] = value
            for k in range(span // 128):
                mass = mass + value[:, k * 128 : (k + 1) * 128]
        return mass

    for d in range(1, n_frame):
        logt_copies[d].wait()
        mass = exponentials(d, mass)
        rest_copies[d].wait()
        for i in range(1, 4):
            rows = rows_of(lax.rem(my_quarter + i, 4))
            away[d - 1, rows] = frames[d, rows].astype(F32).astype(BF16)
        correlation = correlation + lax.dot_general(
            logt[d], away[d - 1], contract, preferred_element_type=F32
        )
    logt_copies[0].wait()
    mass = exponentials(0, mass)
    for c in range(OWN):
        own_copies[c].wait()
        cols = slice(c * own, (c + 1) * own)
        low_counts = frames[0, :, cols].astype(F32).astype(BF16)
        pool[mine, :, cols] = low_counts
        correlation = correlation + lax.dot_general(
            logt[0, :, cols], low_counts, contract, preferred_element_type=F32
        )

    pl.semaphore_wait(hello.at[0], GROUP - 1)
    greet_frames(hello.at[1])

    score = (64.0 / pixels) * (correlation - jnp.sum(mass, axis=1, keepdims=True))
    peak = jnp.max(score, axis=0, keepdims=True)
    grown = jnp.exp(score - peak)
    share_all[mine] = grown.astype(BF16)
    here = mine * n_orient + me
    stat_all[here, 0:1, :] = peak
    stat_all[here, 1:2, :] = jnp.sum(grown, axis=0, keepdims=True)
    share_copies = []
    for d in range(1, n_frame):
        copy = remote(
            share_all.at[mine],
            share_all.at[mine],
            share_send.at[d - 1],
            share_recv.at[d - 1],
            {"frame": lax.rem(mine + d, n_frame)},
        )
        copy.start()
        share_copies.append(copy)
    pl.semaphore_wait(hello.at[1], n_frame - 1)

    def send_stat(d, to):
        remote(
            stat_all.at[here],
            stat_all.at[here],
            fan_send.at[0],
            fan_recv.at[0],
            {"orient": lax.rem(me + d, n_orient), "frame": to},
        ).start()

    for e in range(1, n_frame):
        to = lax.rem(mine + e, n_frame)
        each(far_first(n_orient), lambda d: send_stat(d, to))
        send_stat(0, to)
    each(far_first(n_orient), lambda d: send_stat(d, mine))

    for copy in small_copies:
        copy.wait()
    weight_low = weight_ref[...].astype(BF16).astype(F32)
    index = index_ref[...]
    lane = lax.broadcasted_iota(jnp.int32, (8, 128), 1)
    joint = spread.shape[1] // tile_rows
    strip = joint * tile_rows

    def build(o, carry):
        first = o * strip
        row_id = lax.broadcasted_iota(jnp.int32, (strip, rot_rows), 0) + first
        total = jnp.zeros((strip, rot_rows), F32)
        for j in range(group_blocks):
            value = jnp.where(row_id == index[0, j][None, :], weight_low[0, j][None, :], 0.0)
            value = value + jnp.where(
                row_id == index[1, j][None, :], weight_low[1, j][None, :], 0.0
            )
            narrow = value.astype(BF16)
            total = total + narrow.astype(F32)
            spread[o, :, j * rot_rows : (j + 1) * rot_rows] = narrow
        weight_sum = jnp.sum(total, axis=1, keepdims=True)
        for i in range(joint):
            packed = jnp.zeros((8, 128), F32)
            for b in range(tile_rows // 8):
                at = i * tile_rows + b * 8
                exact = weight_sum[at : at + 8]
                upper = exact.astype(BF16).astype(F32)
                packed = packed + jnp.where(lane == b, upper, 0.0)
                packed = packed + jnp.where(lane == 64 + b, exact - upper, 0.0)
            sums[o * joint + i] = packed.astype(BF16)
        return carry

    builds = n_orient // joint
    lax.fori_loop(0, builds // 2, build, 0)
    relay(0)
    lax.fori_loop(builds // 2, 3 * builds // 4, build, 0)
    relay(1)
    lax.fori_loop(3 * builds // 4, builds, build, 0)

    def send_sums(d):
        to = lax.rem(me + d, n_orient)
        remote(
            sums.at[to], sums_in.at[d - 1], fan_send.at[3], fan_recv.at[3], {"orient": to}
        ).start()

    for k in range(2, CHUNKS):
        relay(k)
    each(far_first(n_orient), send_sums)
    for k in range(2):
        pass_on(k)

    stats_there = stat_all.at[pl.ds(0, n_orient * n_frame - 1)]
    pltpu.make_async_copy(stats_there, stats_there, fan_recv.at[0]).wait()
    for copy in share_copies:
        copy.wait_recv()
    den_all = jnp.zeros((rot_rows, 1), F32)
    for f in range(n_frame):
        peaks = stat_all[f * n_orient : (f + 1) * n_orient, 0, :]
        totals = stat_all[f * n_orient : (f + 1) * n_orient, 1, :]
        peak = jnp.max(peaks, axis=0, keepdims=True)
        total = jnp.sum(totals * jnp.exp(peaks - peak), axis=0, keepdims=True)
        scale = jnp.exp(stat_all[f * n_orient + me, 0:1, :] - peak) / total
        resp = share_all[f].astype(F32) * scale
        resp_all[f] = resp.astype(BF16)
        den_all = den_all + jnp.sum(resp, axis=1, keepdims=True)

        @pl.when(mine == f)
        def _():
            evidence_ref[...] = peak + jnp.log(total)

    share = frame_rows * n_frame / (rot_rows * n_orient)
    inverse = 1.0 / (den_all + share)
    blocks = hop // width

    def process(k):
        cols = slice(k * hop, (k + 1) * hop)
        value = share * intensity[:, cols]
        for f in range(n_frame):
            value = value + jnp.dot(resp_all[f], pool[f, :, cols], preferred_element_type=F32)
        value = value * inverse
        for b in range(blocks):
            j = k * blocks + b
            update[j * rot_rows : (j + 1) * rot_rows] = value[
                :, b * width : (b + 1) * width
            ].astype(BF16)
        deep = slice(k * blocks * rot_rows, (k + 1) * blocks * rot_rows)

        def gather(c, carry):
            block = spread[pl.ds(c * (chunk // strip), chunk // strip), :, deep]
            summed = jnp.dot(
                block.reshape(chunk, blocks * rot_rows), update[deep], preferred_element_type=F32
            )
            if k > 0:
                summed = summed + gathered[c]
            if k < CHUNKS - 1:
                gathered[c] = summed
            else:
                for i in range(chunk // tile_rows):
                    tile_out[c * (chunk // tile_rows) + i] = summed[
                        i * tile_rows : (i + 1) * tile_rows
                    ].astype(BF16)
            return carry

        lax.fori_loop(0, tile_count // chunk, gather, 0)

    pass_on(2)
    arrived(0)
    process(0)
    pass_on(3)
    arrived(1)
    process(1)
    arrived(2)
    process(2)
    arrived(3)
    process(3)

    def send_tiles(d):
        to = lax.rem(me + d, n_orient)
        remote(
            tile_out.at[to], tile_in.at[d - 1], fan_send.at[1], fan_recv.at[1], {"orient": to}
        ).start()

    each(far_first(n_orient), send_tiles)

    prior_weight = rot_rows * group_blocks / (4.0 * tile_rows)
    pltpu.make_async_copy(sums_in, sums_in, fan_recv.at[3]).wait()
    packed = lax.fori_loop(
        0, n_orient - 1, lambda d, so_far: so_far + sums_in[d].astype(F32), sums[me].astype(F32)
    )
    weight = jnp.concatenate(
        [packed[:, b : b + 1] + packed[:, 64 + b : 65 + b] for b in range(tile_rows // 8)], axis=0
    )
    weight = 1.0 / (weight + prior_weight)
    prior = prior_weight * prior_ref[0] + tile_out[me].astype(F32)
    both = weight_low[0] + weight_low[1]
    both = jnp.where(index[0] == index[1], both.astype(BF16).astype(F32), both)
    scale = 1.0 / both

    pltpu.make_async_copy(tile_in, tile_in, fan_recv.at[1]).wait()
    whole = lax.fori_loop(
        0, n_orient - 1, lambda d, so_far: so_far + tile_in[d].astype(F32), prior
    )
    value = whole * weight
    volume_ref[0] = value
    tiles[me] = (value - 1.0).astype(BF16)

    def send_volume(d):
        where = tiles.at[me]
        remote(
            where, where, fan_send.at[2], fan_recv.at[2], {"orient": lax.rem(me + d, n_orient)}
        ).start()

    each(far_first(n_orient), send_volume)

    pltpu.make_async_copy(away, away, count_send.at[0]).wait()
    for copy in share_copies:
        copy.wait_send()
    pltpu.make_async_copy(stats_there, stats_there, fan_send.at[0]).wait()
    pltpu.make_async_copy(sums_in, sums_in, fan_send.at[3]).wait()
    pltpu.make_async_copy(tile_in, tile_in, fan_send.at[1]).wait()
    incoming = tiles.at[pl.ds(0, n_orient - 1)]
    pltpu.make_async_copy(incoming, incoming, fan_recv.at[2]).wait()
    owners = chunk // tile_rows

    def turn(c, carry):
        value = tiles[pl.ds(c * owners, owners)].astype(F32).reshape(chunk, width)
        tiles_t[:, pl.ds(pl.multiple_of(c * chunk, 128), chunk)] = value.T.astype(BF16)
        return carry

    lax.fori_loop(0, tile_count // chunk, turn, 0)
    pair = 2 if group_blocks % 2 == 0 else 1
    for c in range(group_blocks // pair):
        cols = slice(c * pair * rot_rows, (c + 1) * pair * rot_rows)
        block = spread[:, :, cols].reshape(tile_count, pair * rot_rows)
        blended = jnp.dot(tiles_t[...], block, preferred_element_type=F32)
        for k in range(pair):
            j = c * pair + k
            value = blended[:, k * rot_rows : (k + 1) * rot_rows] * scale[j][None, :]
            value = jnp.log(1.0 + value)
            new_log_ref[:, j * width : (j + 1) * width] = value.T.astype(BF16)
    pltpu.make_async_copy(incoming, incoming, fan_send.at[2]).wait()


def place(a_in, b_in, c_in, a_out, b_out, c_out, sem):
    copies = [
        pltpu.make_async_copy(source, target, sem.at[i])
        for i, (source, target) in enumerate(((a_in, a_out), (b_in, b_out), (c_in, c_out)))
    ]
    for copy in copies:
        copy.start()
    for copy in copies:
        copy.wait()


def on_device(log_tomograms, frames, tile_index, tile_weight, prior_volume):
    n_orient = lax.axis_size("orient")
    n_frame = lax.axis_size("frame")
    rot_rows, pixels = log_tomograms.shape
    frame_rows = frames.shape[0]
    group_blocks = tile_index.shape[1]
    tile_rows, width = prior_volume.shape[1:]
    columns = pixels // n_frame
    tile_count = tile_rows * n_orient
    others = max(n_frame - 1, 1)
    chunk = (384 // tile_rows if n_orient % max(384 // tile_rows, 1) == 0 else 1) * tile_rows
    dma = pltpu.SemaphoreType.DMA
    vmem = pl.BlockSpec(memory_space=pltpu.VMEM)
    hbm = pl.BlockSpec(memory_space=pltpu.HBM)
    new_log, volume, evidence = pl.pallas_call(
        functools.partial(kernel, n_orient, n_frame),
        out_shape=(
            pltpu.VMEM((rot_rows, columns), BF16),
            pltpu.VMEM((1, tile_rows, width), F32),
            pltpu.VMEM((1, frame_rows), F32),
        ),
        in_specs=[hbm] * 5,
        out_specs=(vmem, vmem, vmem),
        scratch_shapes=[
            pltpu.VMEM((n_frame, rot_rows, columns), BF16),
            pltpu.VMEM((n_frame, frame_rows, columns), jnp.int32),
            pltpu.VMEM(tile_index.shape, jnp.int32),
            pltpu.VMEM(tile_weight.shape, F32),
            pltpu.VMEM(prior_volume.shape, F32),
            pltpu.VMEM((others, frame_rows, columns), BF16),
            pltpu.VMEM((n_frame, frame_rows, columns), BF16),
            pltpu.VMEM((rot_rows, columns), F32),
            pltpu.VMEM((n_frame, rot_rows, frame_rows), BF16),
            pltpu.VMEM((n_frame * n_orient, 2, frame_rows), F32),
            pltpu.VMEM((n_frame, rot_rows, frame_rows), BF16),
            pltpu.VMEM((n_orient // 2, 2 * tile_rows, group_blocks * rot_rows), BF16),
            pltpu.VMEM((group_blocks * rot_rows, width), BF16),
            pltpu.VMEM((n_orient, 8, width), BF16),
            pltpu.VMEM((n_orient - 1, 8, width), BF16),
            pltpu.VMEM((tile_count // chunk, chunk, width), F32),
            pltpu.VMEM((n_orient, tile_rows, width), BF16),
            pltpu.VMEM((n_orient - 1, tile_rows, width), BF16),
            pltpu.VMEM((n_orient, tile_rows, width), BF16),
            pltpu.VMEM((width, tile_count), BF16),
            dma((5, max(n_frame, 2))),
            pltpu.SemaphoreType.REGULAR((2,)),
            dma((1,)),
            dma((6, others, CHUNKS)),
            dma((others,)),
            dma((others,)),
            dma((4,)),
            dma((4,)),
        ],
        compiler_params=pltpu.CompilerParams(
            collective_id=0, has_side_effects=True, vmem_limit_bytes=48 * 1024 * 1024
        ),
    )(*(
        pltpu.with_memory_space_constraint(value, pltpu.HBM)
        for value in (log_tomograms, frames, tile_index, tile_weight, prior_volume)
    ))
    made = (new_log, volume, evidence)
    new_log, volume, evidence = pl.pallas_call(
        place,
        out_shape=tuple(jax.ShapeDtypeStruct(value.shape, value.dtype) for value in made),
        in_specs=[vmem] * 3,
        out_specs=(hbm,) * 3,
        scratch_shapes=[dma((3,))],
        compiler_params=pltpu.CompilerParams(vmem_limit_bytes=4 * 1024 * 1024),
    )(*made)
    return (new_log, volume, evidence.reshape(frame_rows))


def solution(mesh):
    placed = (
        P("orient", None),
        P("frame", None),
        P(None, "frame", "orient"),
        P(None, "frame", "orient"),
        P("frame", "orient", None),
    )
    return jax.shard_map(
        on_device,
        mesh=mesh,
        in_specs=placed,
        out_specs=(P("orient", "frame"), P("frame", "orient", None), P("frame")),
        check_vma=False,
    )
```

time: 33.2 us -> 30.3 us (0.913)
  Pallas kernels: 32.4 us -> 29.5 us
    pallas_call x1, Pallas kernels: 31.5 us -> 28.7 us  [on_device(): pl.pallas_call(functools.partial(kernel, n_orient, n_frame), out_shape=(p...]
where the time goes in v1:
time: 30.3 us; the launch traced here: 30.1 us
  Pallas kernels  29.5 us (97%)
  between operations  0.64 us (2%)
    pallas_call x1, Pallas kernels, on_device(): pl.pallas_call(functools.partial(kernel, n_orient, n_frame), out_shape=(p...  28.7 us
    pallas_call x1, Pallas kernels, on_device(): pl.pallas_call(place, out_shape=tuple((jax.ShapeDtypeStruct(value.shape,...  0.83 us

profile of v1, /device:TPU:0, one launch (start us, length us, event | category | flops | bytes accessed | tf_op | source)
XLA Modules:
  0.0 30.1 jit_solution(528576770098315227)
XLA Ops:
  0.6 28.7 %shard_map.76 = (bf16[128,2048]{1,0:T(8,128)(2,1)S(1)}, f32[1,24,128]{2,1,0:T(8,128)S(1)}, f32[1,256]{1,0:T(1,128)S(1)}) custom-call(bf16[128,4096]{1,0:T(8,128)(2,1)} %logt_hbm.1, s32[256,4096]{1,0:T(8,128)} %frames_hbm.1, s32[2,16,128]{2,1,0:T(8,128)} %index_hbm.1, f32[2,16,128]{2,1,0:T(8,128)} %weight_hbm.1, f32[1,24,128]{2,1,0:T(8,128)} %prior_hbm.1), custom_call_target="tpu_custom_call" | custom-call | tf_op jit(solution)/shard_map/pallas_call | solution.py:522
  29.3 0.8 %shard_map.77 = (bf16[128,2048]{1,0:T(8,128)(2,1)}, f32[1,24,128]{2,1,0:T(8,128)}, f32[1,256]{1,0:T(1,128)}) custom-call(bf16[128,2048]{1,0:T(8,128)(2,1)S(1)} %get-tuple-element.9.a_in, f32[1,24,128]{2,1,0:T(8,128)S(1)} %get-tuple-element.10.b_in, f32[1,256]{1,0:T(1,128)S(1)} %get-tuple-element.11.c_in), custom_call_target="tpu_custom_call" | custom-call | tf_op jit(solution)/shard_map/pallas_call | solution.py:569

commit v2 on v1

v2 whole, which is shorter than its diff:
```python
import functools

import jax
import jax.numpy as jnp
from jax import lax
from jax.experimental import pallas as pl
from jax.experimental.pallas import tpu as pltpu
from jax.sharding import PartitionSpec as P

MESH = pl.DeviceIdType.MESH
F32 = jnp.float32
BF16 = jnp.bfloat16
GROUP = 8
CHUNKS = 4


def remote(src, dst, send_sem, recv_sem, where):
    return pltpu.make_async_remote_copy(
        src_ref=src,
        dst_ref=dst,
        send_sem=send_sem,
        recv_sem=recv_sem,
        device_id=where,
        device_id_type=MESH,
    )


def far_first(count):
    return sorted(range(1, count), key=lambda d: -min(d, count - d))


def each(order, body):
    if len(order) <= 32:
        for d in order:
            body(d)
    else:

        def step(d, carry):
            body(d)
            return carry

        lax.fori_loop(1, len(order) + 1, step, 0)


def kernel(
    n_orient,
    n_frame,
    logt_hbm,
    frames_hbm,
    index_hbm,
    weight_hbm,
    prior_hbm,
    new_log_ref,
    volume_ref,
    evidence_ref,
    logt,
    logt_pair,
    frames,
    index_ref,
    index_pair,
    weight_ref,
    weight_pair,
    prior_ref,
    away,
    near,
    other,
    intensity,
    share_all,
    stat_all,
    resp_all,
    spread,
    spread_pair,
    update,
    sums,
    sums_in,
    gathered,
    tile_out,
    tile_in,
    tiles,
    tiles_t,
    in_sem,
    hello,
    count_send,
    count_recv,
    pair_send,
    pair_recv,
    share_send,
    share_recv,
    fan_send,
    fan_recv,
):
    me = lax.axis_index("orient")
    mine = lax.axis_index("frame")
    rot_rows = logt.shape[2]
    frame_rows = frames.shape[2]
    group_blocks = index_ref.shape[1]
    half_blocks = group_blocks // 2
    tile_rows, width = prior_ref.shape[1:]
    half = logt.shape[3]
    columns = 2 * half
    pixels = columns * n_frame
    tile_count = tile_rows * n_orient
    chunk = (384 // tile_rows if n_orient % max(384 // tile_rows, 1) == 0 else 1) * tile_rows
    quarter = frame_rows // 4
    hop = half // CHUNKS

    place_in = lax.rem(me, GROUP)
    base = me - place_in
    core = lax.rem(place_in, 2)
    low = lax.rem(place_in // 2, 2)
    high = place_in // 4
    parity = lax.rem(low + high, 2)
    partner = me + 1 - 2 * core
    beside = me + 2 - 4 * low
    above = me + 4 - 8 * high

    barrier = pltpu.get_barrier_semaphore()

    def signal(sem, where):
        pl.semaphore_signal(sem, inc=1, device_id=where, device_id_type=MESH)

    groups = n_orient // GROUP

    def greet_group(sem):
        for e in range(n_frame):
            for i in range(GROUP):
                if e + i > 0:
                    where = base + lax.rem(place_in + i, GROUP)
                    signal(sem, {"orient": where, "frame": lax.rem(mine + e, n_frame)})

    def greet_alike(sem):
        for e in range(n_frame):
            to = lax.rem(mine + e, n_frame)
            each(
                list(range(1, groups)),
                lambda k: signal(
                    sem, {"orient": lax.rem(me + k * GROUP, n_orient), "frame": to}
                ),
            )

    def rows_of(q, count=1):
        return pl.ds(pl.multiple_of(q * quarter, quarter), count * quarter)

    def columns_of(d, side):
        start = lax.rem(mine + d, n_frame) * columns + (core + side - 2 * core * side) * half
        return pl.ds(pl.multiple_of(start, 128), half)

    def source_of(d):
        return lax.rem(mine + n_frame - d, n_frame)

    def load(source, target, sem):
        copy = pltpu.make_async_copy(source, target, sem)
        copy.start()
        return copy

    mine_rows = rows_of(parity * 2, 2)
    rest_rows = rows_of(2 - parity * 2, 2)
    first_copies = [
        load(
            frames_hbm.at[mine_rows, columns_of(d, 0)],
            frames.at[d, 0, mine_rows],
            in_sem.at[0, d - 1],
        )
        for d in range(1, n_frame)
    ]
    greet_alike(barrier)
    greet_group(barrier)

    loads = {}
    for d in (*range(1, n_frame), 0):
        for side in range(2):
            first = load(
                logt_hbm.at[:, columns_of(d, side)], logt.at[d, side], in_sem.at[1 + side, d]
            )
            rows = rest_rows if d > 0 and side == 0 else pl.ds(0, frame_rows)
            rest = load(
                frames_hbm.at[rows, columns_of(d, side)],
                frames.at[d, side, rows],
                in_sem.at[3 + side, d],
            )
            loads[d, side] = (first, rest)
    small_copies = [
        load(index_hbm, index_ref, in_sem.at[5, 0]),
        load(weight_hbm, weight_ref, in_sem.at[5, 1]),
        load(prior_hbm, prior_ref, in_sem.at[0, n_frame - 1]),
    ]

    for d in range(1, n_frame):
        first_copies[d - 1].wait()
        away[d - 1, mine_rows] = frames[d, 0, mine_rows].astype(F32).astype(BF16)

    pl.semaphore_wait(barrier, groups * n_frame - n_frame + GROUP * n_frame - 1)

    relayed = rows_of(parity * 2 + low)
    kept = rows_of(parity * 2 + 1 - low)
    cross = {}

    def part_cols(k):
        return pl.ds(k * hop, hop)

    def send_across(kind, rows):
        for k in range(CHUNKS):
            for d in range(1, n_frame):
                cross[kind, k, d] = remote(
                    away.at[d - 1, rows, part_cols(k)],
                    other.at[d - 1, rows, part_cols(k)],
                    count_send.at[0],
                    count_recv.at[kind, d - 1, k],
                    {"frame": lax.rem(mine + d, n_frame)},
                )
                cross[kind, k, d].start()

    greet_group(hello.at[0])
    send_across(0, relayed)

    def relay(k):
        for d in range(1, n_frame):
            cross[0, k, d].wait_recv()
            where = other.at[d - 1, relayed, part_cols(k)]
            for to in (beside, above):
                remote(
                    where, where, count_send.at[0], count_recv.at[2, d - 1, k], {"orient": to}
                ).start()

    def arrived(k):
        for d in range(1, n_frame):
            where = other.at[d - 1, rest_rows, part_cols(k)]
            pltpu.make_async_copy(where, where, count_recv.at[2, d - 1, k]).wait()
            cross[1, k, d].wait_recv()

    mass = jnp.zeros((rot_rows, 128), F32)
    correlation = jnp.zeros((rot_rows, frame_rows), F32)
    contract = (((1,), (1,)), ((), ()))

    for d in (*range(1, n_frame), 0):
        for side in range(2):
            loads[d, side][0].wait()
            value = jnp.exp(logt[d, side].astype(F32))
            if d == 0 and side == 0:
                intensity[0] = value
            for k in range(half // 128):
                mass = mass + value[:, k * 128 : (k + 1) * 128]
            loads[d, side][1].wait()
            if d > 0 and side == 0:
                away[d - 1, rest_rows] = frames[d, 0, rest_rows].astype(F32).astype(BF16)
                counts = away[d - 1]
            else:
                counts = frames[d, side].astype(F32).astype(BF16)
                if d == 0 and side == 0:
                    near[...] = counts
            correlation = correlation + lax.dot_general(
                logt[d, side], counts, contract, preferred_element_type=F32
            )

    score = (64.0 / pixels) * (correlation - jnp.sum(mass, axis=1, keepdims=True))
    peak = jnp.max(score, axis=0, keepdims=True)
    grown = jnp.exp(score - peak)
    share_all[0, 0] = grown.astype(BF16)
    here = mine * n_orient + me
    stat_all[here, 0:1, :] = peak
    stat_all[here, 1:2, :] = jnp.sum(grown, axis=0, keepdims=True)
    pl.semaphore_wait(hello.at[0], GROUP * n_frame - 1)

    def send_stat(d, to):
        remote(
            stat_all.at[here],
            stat_all.at[here],
            fan_send.at[0],
            fan_recv.at[0],
            {"orient": lax.rem(me + d, n_orient), "frame": to},
        ).start()

    for e in range(1, n_frame):
        to = lax.rem(mine + e, n_frame)
        each(far_first(n_orient), lambda d: send_stat(d, to))
        send_stat(0, to)
    each(far_first(n_orient), lambda d: send_stat(d, mine))

    def send_share(d, side, to):
        copy = remote(
            share_all.at[0 if side == 0 or d == 0 else d, 0],
            share_all.at[d, side],
            share_send.at[d, side],
            share_recv.at[d, side],
            to,
        )
        copy.start()
        return copy

    shares = {
        (d, 0): send_share(d, 0, {"frame": lax.rem(mine + d, n_frame)})
        for d in range(1, n_frame)
    }
    shares[0, 1] = send_share(0, 1, {"orient": partner})
    send_across(1, kept)
    for copy in small_copies:
        copy.wait()
    pair_copies = []
    for i, (source, target) in enumerate(
        ((index_ref, index_pair), (weight_ref, weight_pair), (logt.at[0, 1], logt_pair))
    ):
        copy = remote(source, target, pair_send.at[i], pair_recv.at[i], {"orient": partner})
        copy.start()
        pair_copies.append(copy)

    def swap(value):
        turned = jnp.concatenate([value[:, half_blocks:], value[:, :half_blocks]], axis=1)
        return jnp.where(core == 0, value, turned)

    index = swap(index_ref[...])
    weight_low = swap(weight_ref[...].astype(BF16).astype(F32))
    lane = lax.broadcasted_iota(jnp.int32, (8, 128), 1)
    joint = spread.shape[1] // tile_rows
    strip = joint * tile_rows

    def hits(row_id, index, weight, j):
        value = jnp.where(row_id == index[0, j][None, :], weight[0, j][None, :], 0.0)
        value = value + jnp.where(row_id == index[1, j][None, :], weight[1, j][None, :], 0.0)
        return value.astype(BF16)

    def build(o, carry):
        row_id = lax.broadcasted_iota(jnp.int32, (strip, rot_rows), 0) + o * strip
        total = jnp.zeros((strip, rot_rows), F32)
        for j in range(group_blocks):
            narrow = hits(row_id, index, weight_low, j)
            total = total + narrow.astype(F32)
            spread[o, :, j * rot_rows : (j + 1) * rot_rows] = narrow
        weight_sum = jnp.sum(total, axis=1, keepdims=True)
        for i in range(joint):
            packed = jnp.zeros((8, 128), F32)
            for b in range(tile_rows // 8):
                at = i * tile_rows + b * 8
                exact = weight_sum[at : at + 8]
                upper = exact.astype(BF16).astype(F32)
                packed = packed + jnp.where(lane == b, upper, 0.0)
                packed = packed + jnp.where(lane == 64 + b, exact - upper, 0.0)
            sums[o * joint + i] = packed.astype(BF16)
        return carry

    builds = n_orient // joint
    for k in range(CHUNKS):
        lax.fori_loop(k * builds // CHUNKS, (k + 1) * builds // CHUNKS, build, 0)
        relay(k)

    def send_sums(d):
        to = lax.rem(me + d, n_orient)
        remote(
            sums.at[to], sums_in.at[d - 1], fan_send.at[3], fan_recv.at[3], {"orient": to}
        ).start()

    each(far_first(n_orient), send_sums)

    for copy in pair_copies:
        copy.wait_recv()
    index_two = jnp.where(core == 0, index_pair[:, :half_blocks], index_pair[:, half_blocks:])
    weight_two = jnp.where(core == 0, weight_pair[:, :half_blocks], weight_pair[:, half_blocks:])
    weight_two = weight_two.astype(BF16).astype(F32)
    intensity[1] = jnp.exp(logt_pair[...].astype(F32))

    def build_pair(o, carry):
        row_id = lax.broadcasted_iota(jnp.int32, (strip, rot_rows), 0) + o * strip
        for j in range(half_blocks):
            spread_pair[o, :, j * rot_rows : (j + 1) * rot_rows] = hits(
                row_id, index_two, weight_two, j
            )
        return carry

    lax.fori_loop(0, builds, build_pair, 0)

    for d in range(1, n_frame):
        shares[d, 0].wait_recv()
        shares[d, 1] = send_share(d, 1, {"orient": partner})

    stats_there = stat_all.at[pl.ds(0, n_orient * n_frame - 1)]
    pltpu.make_async_copy(stats_there, stats_there, fan_recv.at[0]).wait()
    shares[0, 1].wait_recv()
    den = [jnp.zeros((rot_rows, 1), F32) for _ in range(2)]
    for d in range(n_frame):
        at = source_of(d) * n_orient
        peaks = stat_all[pl.ds(at, n_orient), 0, :]
        totals = stat_all[pl.ds(at, n_orient), 1, :]
        peak = jnp.max(peaks, axis=0, keepdims=True)
        total = jnp.sum(totals * jnp.exp(peaks - peak), axis=0, keepdims=True)
        if d == 0:
            evidence_ref[...] = peak + jnp.log(total)
        for side, owner in enumerate((me, partner)):
            if d > 0 and side == 1:
                shares[d, 1].wait_recv()
            scale = jnp.exp(stat_all[at + owner, 0:1, :] - peak) / total
            resp = share_all[d, side].astype(F32) * scale
            resp_all[d, side * rot_rows : (side + 1) * rot_rows] = resp.astype(BF16)
            den[side] = den[side] + jnp.sum(resp, axis=1, keepdims=True)

    share = frame_rows * n_frame / (rot_rows * n_orient)
    inverse = [1.0 / (value + share) for value in den]
    blocks = hop // width

    def process(k):
        cols = slice(k * hop, (k + 1) * hop)
        mixed = jnp.dot(resp_all[0], near[:, cols], preferred_element_type=F32)
        for d in range(1, n_frame):
            mixed = mixed + jnp.dot(resp_all[d], other[d - 1, :, cols], preferred_element_type=F32)
        for side in range(2):
            value = mixed[side * rot_rows : (side + 1) * rot_rows] + share * intensity[side, :, cols]
            value = value * inverse[side]
            for b in range(blocks):
                j = k * blocks + b
                update[side, j * rot_rows : (j + 1) * rot_rows] = value[
                    :, b * width : (b + 1) * width
                ].astype(BF16)
        deep = slice(k * blocks * rot_rows, (k + 1) * blocks * rot_rows)

        def gather(c, carry):
            strips = pl.ds(c * (chunk // strip), chunk // strip)
            summed = jnp.dot(
                spread[strips, :, deep].reshape(chunk, blocks * rot_rows),
                update[0, deep],
                preferred_element_type=F32,
            )
            summed = summed + jnp.dot(
                spread_pair[strips, :, deep].reshape(chunk, blocks * rot_rows),
                update[1, deep],
                preferred_element_type=F32,
            )
            if k > 0:
                summed = summed + gathered[c]
            if k < CHUNKS - 1:
                gathered[c] = summed
            else:
                for i in range(chunk // tile_rows):
                    tile_out[c * (chunk // tile_rows) + i] = summed[
                        i * tile_rows : (i + 1) * tile_rows
                    ].astype(BF16)
            return carry

        lax.fori_loop(0, tile_count // chunk, gather, 0)

    for k in range(CHUNKS):
        arrived(k)
        process(k)

    def send_tiles(d):
        to = lax.rem(me + d, n_orient)
        remote(
            tile_out.at[to], tile_in.at[d - 1], fan_send.at[1], fan_recv.at[1], {"orient": to}
        ).start()

    each(far_first(n_orient), send_tiles)

    prior_weight = rot_rows * group_blocks / (4.0 * tile_rows)
    pltpu.make_async_copy(sums_in, sums_in, fan_recv.at[3]).wait()
    packed = lax.fori_loop(
        0, n_orient - 1, lambda d, so_far: so_far + sums_in[d].astype(F32), sums[me].astype(F32)
    )
    weight = jnp.concatenate(
        [packed[:, b : b + 1] + packed[:, 64 + b : 65 + b] for b in range(tile_rows // 8)], axis=0
    )
    weight = 1.0 / (weight + prior_weight)
    prior = prior_weight * prior_ref[0] + tile_out[me].astype(F32)
    both = weight_low[0] + weight_low[1]
    both = jnp.where(index[0] == index[1], both.astype(BF16).astype(F32), both)
    scale = 1.0 / both
    for copy in pair_copies:
        copy.wait_send()
    pltpu.make_async_copy(other, other, count_send.at[0]).wait()
    for copy in shares.values():
        copy.wait_send()
    pltpu.make_async_copy(stats_there, stats_there, fan_send.at[0]).wait()
    pltpu.make_async_copy(sums_in, sums_in, fan_send.at[3]).wait()

    pltpu.make_async_copy(tile_in, tile_in, fan_recv.at[1]).wait()
    whole = lax.fori_loop(
        0, n_orient - 1, lambda d, so_far: so_far + tile_in[d].astype(F32), prior
    )
    value = whole * weight
    volume_ref[0] = value
    tiles[me] = (value - 1.0).astype(BF16)

    def send_volume(d):
        where = tiles.at[me]
        remote(
            where, where, fan_send.at[2], fan_recv.at[2], {"orient": lax.rem(me + d, n_orient)}
        ).start()

    each(far_first(n_orient), send_volume)

    pltpu.make_async_copy(tile_in, tile_in, fan_send.at[1]).wait()
    incoming = tiles.at[pl.ds(0, n_orient - 1)]
    pltpu.make_async_copy(incoming, incoming, fan_recv.at[2]).wait()
    owners = chunk // tile_rows

    def turn(c, carry):
        value = tiles[pl.ds(c * owners, owners)].astype(F32).reshape(chunk, width)
        tiles_t[:, pl.ds(pl.multiple_of(c * chunk, 128), chunk)] = value.T.astype(BF16)
        return carry

    lax.fori_loop(0, tile_count // chunk, turn, 0)
    pair = 2 if half_blocks % 2 == 0 else 1
    for c in range(group_blocks // pair):
        cols = slice(c * pair * rot_rows, (c + 1) * pair * rot_rows)
        block = spread[:, :, cols].reshape(tile_count, pair * rot_rows)
        blended = jnp.dot(tiles_t[...], block, preferred_element_type=F32)
        for k in range(pair):
            j = c * pair + k
            value = blended[:, k * rot_rows : (k + 1) * rot_rows] * scale[j][None, :]
            value = jnp.log(1.0 + value)
            where = lax.rem(core * half_blocks + j, group_blocks) * width
            new_log_ref[:, pl.ds(pl.multiple_of(where, 128), width)] = value.T.astype(BF16)
    pltpu.make_async_copy(incoming, incoming, fan_send.at[2]).wait()


def place(a_in, b_in, c_in, a_out, b_out, c_out, sem):
    copies = [
        pltpu.make_async_copy(source, target, sem.at[i])
        for i, (source, target) in enumerate(((a_in, a_out), (b_in, b_out), (c_in, c_out)))
    ]
    for copy in copies:
        copy.start()
    for copy in copies:
        copy.wait()


def on_device(log_tomograms, frames, tile_index, tile_weight, prior_volume):
    n_orient = lax.axis_size("orient")
    n_frame = lax.axis_size("frame")
    rot_rows, pixels = log_tomograms.shape
    frame_rows = frames.shape[0]
    group_blocks = tile_index.shape[1]
    tile_rows, width = prior_volume.shape[1:]
    columns = pixels // n_frame
    tile_count = tile_rows * n_orient
    others = max(n_frame - 1, 1)
    half = columns // 2
    chunk = (384 // tile_rows if n_orient % max(384 // tile_rows, 1) == 0 else 1) * tile_rows
    dma = pltpu.SemaphoreType.DMA
    vmem = pl.BlockSpec(memory_space=pltpu.VMEM)
    hbm = pl.BlockSpec(memory_space=pltpu.HBM)
    new_log, volume, evidence = pl.pallas_call(
        functools.partial(kernel, n_orient, n_frame),
        out_shape=(
            pltpu.VMEM((rot_rows, columns), BF16),
            pltpu.VMEM((1, tile_rows, width), F32),
            pltpu.VMEM((1, frame_rows), F32),
        ),
        in_specs=[hbm] * 5,
        out_specs=(vmem, vmem, vmem),
        scratch_shapes=[
            pltpu.VMEM((n_frame, 2, rot_rows, half), BF16),
            pltpu.VMEM((rot_rows, half), BF16),
            pltpu.VMEM((n_frame, 2, frame_rows, half), jnp.int32),
            pltpu.VMEM(tile_index.shape, jnp.int32),
            pltpu.VMEM(tile_index.shape, jnp.int32),
            pltpu.VMEM(tile_weight.shape, F32),
            pltpu.VMEM(tile_weight.shape, F32),
            pltpu.VMEM(prior_volume.shape, F32),
            pltpu.VMEM((others, frame_rows, half), BF16),
            pltpu.VMEM((frame_rows, half), BF16),
            pltpu.VMEM((others, frame_rows, half), BF16),
            pltpu.VMEM((2, rot_rows, half), F32),
            pltpu.VMEM((n_frame, 2, rot_rows, frame_rows), BF16),
            pltpu.VMEM((n_frame * n_orient, 2, frame_rows), F32),
            pltpu.VMEM((n_frame, 2 * rot_rows, frame_rows), BF16),
            pltpu.VMEM((n_orient // 2, 2 * tile_rows, group_blocks * rot_rows), BF16),
            pltpu.VMEM((n_orient // 2, 2 * tile_rows, group_blocks // 2 * rot_rows), BF16),
            pltpu.VMEM((2, group_blocks // 2 * rot_rows, width), BF16),
            pltpu.VMEM((n_orient, 8, width), BF16),
            pltpu.VMEM((n_orient - 1, 8, width), BF16),
            pltpu.VMEM((tile_count // chunk, chunk, width), F32),
            pltpu.VMEM((n_orient, tile_rows, width), BF16),
            pltpu.VMEM((n_orient - 1, tile_rows, width), BF16),
            pltpu.VMEM((n_orient, tile_rows, width), BF16),
            pltpu.VMEM((width, tile_count), BF16),
            dma((6, max(n_frame, 2))),
            pltpu.SemaphoreType.REGULAR((1,)),
            dma((1,)),
            dma((3, others, CHUNKS)),
            dma((3,)),
            dma((3,)),
            dma((n_frame, 2)),
            dma((n_frame, 2)),
            dma((4,)),
            dma((4,)),
        ],
        compiler_params=pltpu.CompilerParams(
            collective_id=0, has_side_effects=True, vmem_limit_bytes=48 * 1024 * 1024
        ),
    )(*(
        pltpu.with_memory_space_constraint(value, pltpu.HBM)
        for value in (log_tomograms, frames, tile_index, tile_weight, prior_volume)
    ))
    made = (new_log, volume, evidence)
    new_log, volume, evidence = pl.pallas_call(
        place,
        out_shape=tuple(jax.ShapeDtypeStruct(value.shape, value.dtype) for value in made),
        in_specs=[vmem] * 3,
        out_specs=(hbm,) * 3,
        scratch_shapes=[dma((3,))],
        compiler_params=pltpu.CompilerParams(vmem_limit_bytes=4 * 1024 * 1024),
    )(*made)
    return (new_log, volume, evidence.reshape(frame_rows))


def solution(mesh):
    placed = (
        P("orient", None),
        P("frame", None),
        P(None, "frame", "orient"),
        P(None, "frame", "orient"),
        P("frame", "orient", None),
    )
    return jax.shard_map(
        on_device,
        mesh=mesh,
        in_specs=placed,
        out_specs=(P("orient", "frame"), P("frame", "orient", None), P("frame")),
        check_vma=False,
    )
```

time: 30.3 us -> 28.7 us (0.947)
  Pallas kernels: 29.5 us -> 27.9 us
    pallas_call x1, Pallas kernels: 28.7 us -> 27.1 us  [on_device(): pl.pallas_call(functools.partial(kernel, n_orient, n_frame), out_shape=(p...]
where the time goes in v2:
time: 28.7 us; the launch traced here: 28.5 us
  Pallas kernels  27.9 us (97%)
  between operations  0.64 us (2%)
    pallas_call x1, Pallas kernels, on_device(): pl.pallas_call(functools.partial(kernel, n_orient, n_frame), out_shape=(p...  27.1 us
    pallas_call x1, Pallas kernels, on_device(): pl.pallas_call(place, out_shape=tuple((jax.ShapeDtypeStruct(value.shape,...  0.83 us

profile of v2, /device:TPU:0, one launch (start us, length us, event | category | flops | bytes accessed | tf_op | source)
XLA Modules:
  0.0 28.5 jit_solution(9993040429665833311)
XLA Ops:
  0.6 27.1 %shard_map.76 = (bf16[128,2048]{1,0:T(8,128)(2,1)S(1)}, f32[1,24,128]{2,1,0:T(8,128)S(1)}, f32[1,256]{1,0:T(1,128)S(1)}) custom-call(bf16[128,4096]{1,0:T(8,128)(2,1)} %logt_hbm.1, s32[256,4096]{1,0:T(8,128)} %frames_hbm.1, s32[2,16,128]{2,1,0:T(8,128)} %index_hbm.1, f32[2,16,128]{2,1,0:T(8,128)} %weight_hbm.1, f32[1,24,128]{2,1,0:T(8,128)} %prior_hbm.1), custom_call_target="tpu_custom_call" | custom-call | tf_op jit(solution)/shard_map/pallas_call | solution.py:538
  27.7 0.8 %shard_map.77 = (bf16[128,2048]{1,0:T(8,128)(2,1)}, f32[1,24,128]{2,1,0:T(8,128)}, f32[1,256]{1,0:T(1,128)}) custom-call(bf16[128,2048]{1,0:T(8,128)(2,1)S(1)} %get-tuple-element.9.a_in, f32[1,24,128]{2,1,0:T(8,128)S(1)} %get-tuple-element.10.b_in, f32[1,256]{1,0:T(1,128)S(1)} %get-tuple-element.11.c_in), custom_call_target="tpu_custom_call" | custom-call | tf_op jit(solution)/shard_map/pallas_call | solution.py:592

commit v3 on v2

--- a/solution.py
+++ b/solution.py
@@ -11,7 +11,7 @@
 F32 = jnp.float32
 BF16 = jnp.bfloat16
 GROUP = 8
-CHUNKS = 4
+CHUNKS = 2
 
 
 def remote(src, dst, send_sem, recv_sem, where):
@@ -253,29 +253,12 @@
             )
 
     score = (64.0 / pixels) * (correlation - jnp.sum(mass, axis=1, keepdims=True))
-    peak = jnp.max(score, axis=0, keepdims=True)
-    grown = jnp.exp(score - peak)
+    peak = jnp.max(score, axis=0, keepdims=True).astype(BF16)
+    grown = jnp.exp(score - peak.astype(F32))
     share_all[0, 0] = grown.astype(BF16)
     here = mine * n_orient + me
-    stat_all[here, 0:1, :] = peak
-    stat_all[here, 1:2, :] = jnp.sum(grown, axis=0, keepdims=True)
-    pl.semaphore_wait(hello.at[0], GROUP * n_frame - 1)
-
-    def send_stat(d, to):
-        remote(
-            stat_all.at[here],
-            stat_all.at[here],
-            fan_send.at[0],
-            fan_recv.at[0],
-            {"orient": lax.rem(me + d, n_orient), "frame": to},
-        ).start()
-
-    for e in range(1, n_frame):
-        to = lax.rem(mine + e, n_frame)
-        each(far_first(n_orient), lambda d: send_stat(d, to))
-        send_stat(0, to)
-    each(far_first(n_orient), lambda d: send_stat(d, mine))
-
+    total = jnp.sum(grown, axis=0, keepdims=True).astype(BF16)
+    stat_all[here] = jnp.concatenate([peak, total], axis=0)
     def send_share(d, side, to):
         copy = remote(
             share_all.at[0 if side == 0 or d == 0 else d, 0],
@@ -292,6 +275,23 @@
         for d in range(1, n_frame)
     }
     shares[0, 1] = send_share(0, 1, {"orient": partner})
+    pl.semaphore_wait(hello.at[0], GROUP * n_frame - 1)
+
+    def send_stat(d, to):
+        remote(
+            stat_all.at[here],
+            stat_all.at[here],
+            fan_send.at[0],
+            fan_recv.at[0],
+            {"orient": lax.rem(me + d, n_orient), "frame": to},
+        ).start()
+
+    for e in range(1, n_frame):
+        to = lax.rem(mine + e, n_frame)
+        each(far_first(n_orient), lambda d: send_stat(d, to))
+        send_stat(0, to)
+    each(far_first(n_orient), lambda d: send_stat(d, mine))
+
     send_across(1, kept)
     for copy in small_copies:
         copy.wait()
@@ -377,8 +377,9 @@
     den = [jnp.zeros((rot_rows, 1), F32) for _ in range(2)]
     for d in range(n_frame):
         at = source_of(d) * n_orient
-        peaks = stat_all[pl.ds(at, n_orient), 0, :]
-        totals = stat_all[pl.ds(at, n_orient), 1, :]
+        stats = stat_all[pl.ds(at, n_orient)].astype(F32)
+        peaks = stats[:, 0, :]
+        totals = stats[:, 1, :]
         peak = jnp.max(peaks, axis=0, keepdims=True)
         total = jnp.sum(totals * jnp.exp(peaks - peak), axis=0, keepdims=True)
         if d == 0:
@@ -386,7 +387,7 @@
         for side, owner in enumerate((me, partner)):
             if d > 0 and side == 1:
                 shares[d, 1].wait_recv()
-            scale = jnp.exp(stat_all[at + owner, 0:1, :] - peak) / total
+            scale = jnp.exp(stat_all[at + owner].astype(F32)[0:1] - peak) / total
             resp = share_all[d, side].astype(F32) * scale
             resp_all[d, side * rot_rows : (side + 1) * rot_rows] = resp.astype(BF16)
             den[side] = den[side] + jnp.sum(resp, axis=1, keepdims=True)
@@ -395,7 +396,7 @@
     inverse = [1.0 / (value + share) for value in den]
     blocks = hop // width
 
-    def process(k):
+    def spread_out(k):
         cols = slice(k * hop, (k + 1) * hop)
         mixed = jnp.dot(resp_all[0], near[:, cols], preferred_element_type=F32)
         for d in range(1, n_frame):
@@ -408,44 +409,64 @@
                 update[side, j * rot_rows : (j + 1) * rot_rows] = value[
                     :, b * width : (b + 1) * width
                 ].astype(BF16)
+
+    section = GROUP * tile_rows
+    strips = section // strip
+
+    def gather(k, c):
         deep = slice(k * blocks * rot_rows, (k + 1) * blocks * rot_rows)
-
-        def gather(c, carry):
-            strips = pl.ds(c * (chunk // strip), chunk // strip)
-            summed = jnp.dot(
-                spread[strips, :, deep].reshape(chunk, blocks * rot_rows),
-                update[0, deep],
-                preferred_element_type=F32,
-            )
-            summed = summed + jnp.dot(
-                spread_pair[strips, :, deep].reshape(chunk, blocks * rot_rows),
-                update[1, deep],
-                preferred_element_type=F32,
-            )
-            if k > 0:
-                summed = summed + gathered[c]
-            if k < CHUNKS - 1:
-                gathered[c] = summed
-            else:
-                for i in range(chunk // tile_rows):
-                    tile_out[c * (chunk // tile_rows) + i] = summed[
-                        i * tile_rows : (i + 1) * tile_rows
-                    ].astype(BF16)
-            return carry
-
-        lax.fori_loop(0, tile_count // chunk, gather, 0)
-
-    for k in range(CHUNKS):
+        here = pl.ds(c * strips, strips)
+        summed = jnp.dot(
+            spread[here, :, deep].reshape(section, blocks * rot_rows),
+            update[0, deep],
+            preferred_element_type=F32,
+        )
+        return summed + jnp.dot(
+            spread_pair[here, :, deep].reshape(section, blocks * rot_rows),
+            update[1, deep],
+            preferred_element_type=F32,
+        )
+
+    def keep(k, c):
+        gathered[c] = gather(k, c) if k == 0 else gathered[c] + gather(k, c)
+
+    def finish(away_by, own):
+        c = lax.rem(me // GROUP + away_by, groups)
+        summed = gather(CHUNKS - 1, c)
+        if CHUNKS > 1:
+            summed = summed + gathered[c]
+        for i in range(GROUP):
+            tile_out[c * GROUP + i] = summed[i * tile_rows : (i + 1) * tile_rows].astype(BF16)
+        for i in range(1 if own else 0, GROUP):
+            to = c * GROUP + lax.rem(place_in + i, GROUP)
+            remote(
+                tile_out.at[to],
+                tile_in.at[lax.rem(to - me + n_orient, n_orient) - 1],
+                fan_send.at[1],
+                fan_recv.at[1],
+                {"orient": to},
+            ).start()
+
+    def sections(body):
+        if groups <= 4:
+            for c in range(groups):
+                body(c)
+        else:
+
+            def step(c, carry):
+                body(c)
+                return carry
+
+            lax.fori_loop(0, groups, step, 0)
+
+    arrived(0)
+    spread_out(0)
+    for k in range(1, CHUNKS):
         arrived(k)
-        process(k)
-
-    def send_tiles(d):
-        to = lax.rem(me + d, n_orient)
-        remote(
-            tile_out.at[to], tile_in.at[d - 1], fan_send.at[1], fan_recv.at[1], {"orient": to}
-        ).start()
-
-    each(far_first(n_orient), send_tiles)
+        spread_out(k)
+        sections(lambda c: keep(k - 1, c))
+    each(list(range(1, groups)), lambda c: finish(c, False))
+    finish(0, True)
 
     prior_weight = rot_rows * group_blocks / (4.0 * tile_rows)
     pltpu.make_async_copy(sums_in, sums_in, fan_recv.at[3]).wait()
@@ -558,14 +579,14 @@
             pltpu.VMEM((others, frame_rows, half), BF16),
             pltpu.VMEM((2, rot_rows, half), F32),
             pltpu.VMEM((n_frame, 2, rot_rows, frame_rows), BF16),
-            pltpu.VMEM((n_frame * n_orient, 2, frame_rows), F32),
+            pltpu.VMEM((n_frame * n_orient, 2, frame_rows), BF16),
             pltpu.VMEM((n_frame, 2 * rot_rows, frame_rows), BF16),
             pltpu.VMEM((n_orient // 2, 2 * tile_rows, group_blocks * rot_rows), BF16),
             pltpu.VMEM((n_orient // 2, 2 * tile_rows, group_blocks // 2 * rot_rows), BF16),
             pltpu.VMEM((2, group_blocks // 2 * rot_rows, width), BF16),
             pltpu.VMEM((n_orient, 8, width), BF16),
             pltpu.VMEM((n_orient - 1, 8, width), BF16),
-            pltpu.VMEM((tile_count // chunk, chunk, width), F32),
+            pltpu.VMEM((n_orient // GROUP, GROUP * tile_rows, width), F32),
             pltpu.VMEM((n_orient, tile_rows, width), BF16),
             pltpu.VMEM((n_orient - 1, tile_rows, width), BF16),
             pltpu.VMEM((n_orient, tile_rows, width), BF16),

time: 28.7 us -> 27.5 us (0.958)
  Pallas kernels: 27.9 us -> 26.8 us
    pallas_call x1, Pallas kernels: 27.1 us -> 25.9 us  [on_device(): pl.pallas_call(functools.partial(kernel, n_orient, n_frame), out_shape=(p...]
where the time goes in v3:
time: 27.5 us; the launch traced here: 27.4 us
  Pallas kernels  26.8 us (97%)
  between operations  0.64 us (2%)
    pallas_call x1, Pallas kernels, on_device(): pl.pallas_call(functools.partial(kernel, n_orient, n_frame), out_shape=(p...  25.9 us
    pallas_call x1, Pallas kernels, on_device(): pl.pallas_call(place, out_shape=tuple((jax.ShapeDtypeStruct(value.shape,...  0.83 us

profile of v3, /device:TPU:0, one launch (start us, length us, event | category | flops | bytes accessed | tf_op | source)
XLA Modules:
  0.0 27.4 jit_solution(5848904877063459835)
XLA Ops:
  0.6 25.9 %shard_map.76 = (bf16[128,2048]{1,0:T(8,128)(2,1)S(1)}, f32[1,24,128]{2,1,0:T(8,128)S(1)}, f32[1,256]{1,0:T(1,128)S(1)}) custom-call(bf16[128,4096]{1,0:T(8,128)(2,1)} %logt_hbm.1, s32[256,4096]{1,0:T(8,128)} %frames_hbm.1, s32[2,16,128]{2,1,0:T(8,128)} %index_hbm.1, f32[2,16,128]{2,1,0:T(8,128)} %weight_hbm.1, f32[1,24,128]{2,1,0:T(8,128)} %prior_hbm.1), custom_call_target="tpu_custom_call" | custom-call | tf_op jit(solution)/shard_map/pallas_call | solution.py:559
  26.6 0.8 %shard_map.77 = (bf16[128,2048]{1,0:T(8,128)(2,1)}, f32[1,24,128]{2,1,0:T(8,128)}, f32[1,256]{1,0:T(1,128)}) custom-call(bf16[128,2048]{1,0:T(8,128)(2,1)S(1)} %get-tuple-element.9.a_in, f32[1,24,128]{2,1,0:T(8,128)S(1)} %get-tuple-element.10.b_in, f32[1,256]{1,0:T(1,128)S(1)} %get-tuple-element.11.c_in), custom_call_target="tpu_custom_call" | custom-call | tf_op jit(solution)/shard_map/pallas_call | solution.py:613

commit v4 on v3

--- a/solution.py
+++ b/solution.py
@@ -23,10 +23,6 @@
         device_id=where,
         device_id_type=MESH,
     )
-
-
-def far_first(count):
-    return sorted(range(1, count), key=lambda d: -min(d, count - d))
 
 
 def each(order, body):
@@ -82,9 +78,7 @@
     hello,
     count_send,
     count_recv,
-    pair_send,
     pair_recv,
-    share_send,
     share_recv,
     fan_send,
     fan_recv,
@@ -122,10 +116,10 @@
     groups = n_orient // GROUP
 
     def greet_group(sem):
-        for e in range(n_frame):
-            for i in range(GROUP):
-                if e + i > 0:
-                    where = base + lax.rem(place_in + i, GROUP)
+        for e in reversed(range(n_frame)):
+            for bits in reversed(range(GROUP)):
+                if e + bits > 0:
+                    where = base + flip(bits)
                     signal(sem, {"orient": where, "frame": lax.rem(mine + e, n_frame)})
 
     def greet_alike(sem):
@@ -137,6 +131,26 @@
                     sem, {"orient": lax.rem(me + k * GROUP, n_orient), "frame": to}
                 ),
             )
+
+    def flip(bits):
+        return (
+            (1 - core if bits % 2 else core)
+            + 2 * (1 - low if bits // 2 % 2 else low)
+            + 4 * (1 - high if bits // 4 else high)
+        )
+
+    def to_group(g, body):
+        first = lax.rem(me // GROUP + g, groups) * GROUP
+        for bits in reversed(range(GROUP)):
+            if not (isinstance(g, int) and g == 0 and bits == 0):
+                body(first + flip(bits))
+
+    def to_peers(body):
+        each(list(range(1, groups)), lambda g: to_group(g, body))
+        to_group(0, body)
+
+    def slot_of(to):
+        return lax.rem(to - me + n_orient, n_orient) - 1
 
     def rows_of(q, count=1):
         return pl.ds(pl.multiple_of(q * quarter, quarter), count * quarter)
@@ -263,7 +277,7 @@
         copy = remote(
             share_all.at[0 if side == 0 or d == 0 else d, 0],
             share_all.at[d, side],
-            share_send.at[d, side],
+            in_sem.at[3 + side, d],
             share_recv.at[d, side],
             to,
         )
@@ -277,20 +291,20 @@
     shares[0, 1] = send_share(0, 1, {"orient": partner})
     pl.semaphore_wait(hello.at[0], GROUP * n_frame - 1)
 
-    def send_stat(d, to):
+    def send_stat(to, frame):
         remote(
             stat_all.at[here],
             stat_all.at[here],
             fan_send.at[0],
             fan_recv.at[0],
-            {"orient": lax.rem(me + d, n_orient), "frame": to},
+            {"orient": to, "frame": frame},
         ).start()
 
     for e in range(1, n_frame):
-        to = lax.rem(mine + e, n_frame)
-        each(far_first(n_orient), lambda d: send_stat(d, to))
-        send_stat(0, to)
-    each(far_first(n_orient), lambda d: send_stat(d, mine))
+        frame = lax.rem(mine + e, n_frame)
+        to_peers(lambda to: send_stat(to, frame))
+        send_stat(me, frame)
+    to_peers(lambda to: send_stat(to, mine))
 
     send_across(1, kept)
     for copy in small_copies:
@@ -299,7 +313,7 @@
     for i, (source, target) in enumerate(
         ((index_ref, index_pair), (weight_ref, weight_pair), (logt.at[0, 1], logt_pair))
     ):
-        copy = remote(source, target, pair_send.at[i], pair_recv.at[i], {"orient": partner})
+        copy = remote(source, target, in_sem.at[i + 1, 0], pair_recv.at[i], {"orient": partner})
         copy.start()
         pair_copies.append(copy)
 
@@ -342,13 +356,12 @@
         lax.fori_loop(k * builds // CHUNKS, (k + 1) * builds // CHUNKS, build, 0)
         relay(k)
 
-    def send_sums(d):
-        to = lax.rem(me + d, n_orient)
+    def send_sums(to):
         remote(
-            sums.at[to], sums_in.at[d - 1], fan_send.at[3], fan_recv.at[3], {"orient": to}
+            sums.at[to], sums_in.at[slot_of(to)], fan_send.at[3], fan_recv.at[3], {"orient": to}
         ).start()
 
-    each(far_first(n_orient), send_sums)
+    to_peers(send_sums)
 
     for copy in pair_copies:
         copy.wait_recv()
@@ -430,22 +443,23 @@
     def keep(k, c):
         gathered[c] = gather(k, c) if k == 0 else gathered[c] + gather(k, c)
 
-    def finish(away_by, own):
+    def finish(away_by):
         c = lax.rem(me // GROUP + away_by, groups)
         summed = gather(CHUNKS - 1, c)
         if CHUNKS > 1:
             summed = summed + gathered[c]
         for i in range(GROUP):
             tile_out[c * GROUP + i] = summed[i * tile_rows : (i + 1) * tile_rows].astype(BF16)
-        for i in range(1 if own else 0, GROUP):
-            to = c * GROUP + lax.rem(place_in + i, GROUP)
+        def send_tiles(to):
             remote(
                 tile_out.at[to],
-                tile_in.at[lax.rem(to - me + n_orient, n_orient) - 1],
+                tile_in.at[slot_of(to)],
                 fan_send.at[1],
                 fan_recv.at[1],
                 {"orient": to},
             ).start()
+
+        to_group(away_by, send_tiles)
 
     def sections(body):
         if groups <= 4:
@@ -465,8 +479,8 @@
         arrived(k)
         spread_out(k)
         sections(lambda c: keep(k - 1, c))
-    each(list(range(1, groups)), lambda c: finish(c, False))
-    finish(0, True)
+    each(list(range(1, groups)), finish)
+    finish(0)
 
     prior_weight = rot_rows * group_blocks / (4.0 * tile_rows)
     pltpu.make_async_copy(sums_in, sums_in, fan_recv.at[3]).wait()
@@ -497,13 +511,11 @@
     volume_ref[0] = value
     tiles[me] = (value - 1.0).astype(BF16)
 
-    def send_volume(d):
+    def send_volume(to):
         where = tiles.at[me]
-        remote(
-            where, where, fan_send.at[2], fan_recv.at[2], {"orient": lax.rem(me + d, n_orient)}
-        ).start()
-
-    each(far_first(n_orient), send_volume)
+        remote(where, where, fan_send.at[2], fan_recv.at[2], {"orient": to}).start()
+
+    to_peers(send_volume)
 
     pltpu.make_async_copy(tile_in, tile_in, fan_send.at[1]).wait()
     incoming = tiles.at[pl.ds(0, n_orient - 1)]
@@ -596,8 +608,6 @@
             dma((1,)),
             dma((3, others, CHUNKS)),
             dma((3,)),
-            dma((3,)),
-            dma((n_frame, 2)),
             dma((n_frame, 2)),
             dma((4,)),
             dma((4,)),

time: 27.5 us -> 27 us (0.982)
  Pallas kernels: 26.8 us -> 26.2 us
    pallas_call x1, Pallas kernels: 25.9 us -> 25.3 us  [on_device(): pl.pallas_call(functools.partial(kernel, n_orient, n_frame), out_shape=(p...]
where the time goes in v4:
time: 27 us; the launch traced here: 26.8 us
  Pallas kernels  26.2 us (97%)
  between operations  0.64 us (2%)
    pallas_call x1, Pallas kernels, on_device(): pl.pallas_call(functools.partial(kernel, n_orient, n_frame), out_shape=(p...  25.3 us
    pallas_call x1, Pallas kernels, on_device(): pl.pallas_call(place, out_shape=tuple((jax.ShapeDtypeStruct(value.shape,...  0.83 us

profile of v4, /device:TPU:0, one launch (start us, length us, event | category | flops | bytes accessed | tf_op | source)
XLA Modules:
  0.0 26.8 jit_solution(4202504482525107480)
XLA Ops:
  0.6 25.3 %shard_map.76 = (bf16[128,2048]{1,0:T(8,128)(2,1)S(1)}, f32[1,24,128]{2,1,0:T(8,128)S(1)}, f32[1,256]{1,0:T(1,128)S(1)}) custom-call(bf16[128,4096]{1,0:T(8,128)(2,1)} %logt_hbm.1, s32[256,4096]{1,0:T(8,128)} %frames_hbm.1, s32[2,16,128]{2,1,0:T(8,128)} %index_hbm.1, f32[2,16,128]{2,1,0:T(8,128)} %weight_hbm.1, f32[1,24,128]{2,1,0:T(8,128)} %prior_hbm.1), custom_call_target="tpu_custom_call" | custom-call | tf_op jit(solution)/shard_map/pallas_call | solution.py:571
  26.0 0.8 %shard_map.77 = (bf16[128,2048]{1,0:T(8,128)(2,1)}, f32[1,24,128]{2,1,0:T(8,128)}, f32[1,256]{1,0:T(1,128)}) custom-call(bf16[128,2048]{1,0:T(8,128)(2,1)S(1)} %get-tuple-element.9.a_in, f32[1,24,128]{2,1,0:T(8,128)S(1)} %get-tuple-element.10.b_in, f32[1,256]{1,0:T(1,128)S(1)} %get-tuple-element.11.c_in), custom_call_target="tpu_custom_call" | custom-call | tf_op jit(solution)/shard_map/pallas_call | solution.py:623

commit v5 on v4

--- a/solution.py
+++ b/solution.py
@@ -12,6 +12,7 @@
 BF16 = jnp.bfloat16
 GROUP = 8
 CHUNKS = 2
+FIRST = 10
 
 
 def remote(src, dst, send_sem, recv_sem, where):
@@ -96,7 +97,8 @@
     tile_count = tile_rows * n_orient
     chunk = (384 // tile_rows if n_orient % max(384 // tile_rows, 1) == 0 else 1) * tile_rows
     quarter = frame_rows // 4
-    hop = half // CHUNKS
+    first_part = -(-half * FIRST // (16 * 128)) * 128
+    edges = (0, first_part, half)
 
     place_in = lax.rem(me, GROUP)
     base = me - place_in
@@ -210,7 +212,7 @@
     cross = {}
 
     def part_cols(k):
-        return pl.ds(k * hop, hop)
+        return pl.ds(edges[k], edges[k + 1] - edges[k])
 
     def send_across(kind, rows):
         for k in range(CHUNKS):
@@ -407,18 +409,17 @@
 
     share = frame_rows * n_frame / (rot_rows * n_orient)
     inverse = [1.0 / (value + share) for value in den]
-    blocks = hop // width
 
     def spread_out(k):
-        cols = slice(k * hop, (k + 1) * hop)
+        cols = slice(edges[k], edges[k + 1])
         mixed = jnp.dot(resp_all[0], near[:, cols], preferred_element_type=F32)
         for d in range(1, n_frame):
             mixed = mixed + jnp.dot(resp_all[d], other[d - 1, :, cols], preferred_element_type=F32)
         for side in range(2):
             value = mixed[side * rot_rows : (side + 1) * rot_rows] + share * intensity[side, :, cols]
             value = value * inverse[side]
-            for b in range(blocks):
-                j = k * blocks + b
+            for b in range((edges[k + 1] - edges[k]) // width):
+                j = edges[k] // width + b
                 update[side, j * rot_rows : (j + 1) * rot_rows] = value[
                     :, b * width : (b + 1) * width
                 ].astype(BF16)
@@ -427,15 +428,16 @@
     strips = section // strip
 
     def gather(k, c):
-        deep = slice(k * blocks * rot_rows, (k + 1) * blocks * rot_rows)
+        deep = slice(edges[k] // width * rot_rows, edges[k + 1] // width * rot_rows)
+        depth = deep.stop - deep.start
         here = pl.ds(c * strips, strips)
         summed = jnp.dot(
-            spread[here, :, deep].reshape(section, blocks * rot_rows),
+            spread[here, :, deep].reshape(section, depth),
             update[0, deep],
             preferred_element_type=F32,
         )
         return summed + jnp.dot(
-            spread_pair[here, :, deep].reshape(section, blocks * rot_rows),
+            spread_pair[here, :, deep].reshape(section, depth),
             update[1, deep],
             preferred_element_type=F32,
         )
@@ -504,9 +506,12 @@
     pltpu.make_async_copy(sums_in, sums_in, fan_send.at[3]).wait()
 
     pltpu.make_async_copy(tile_in, tile_in, fan_recv.at[1]).wait()
-    whole = lax.fori_loop(
-        0, n_orient - 1, lambda d, so_far: so_far + tile_in[d].astype(F32), prior
-    )
+    if n_orient <= 32:
+        whole = prior + jnp.sum(tile_in[...].astype(F32), axis=0)
+    else:
+        whole = lax.fori_loop(
+            0, n_orient - 1, lambda d, so_far: so_far + tile_in[d].astype(F32), prior
+        )
     value = whole * weight
     volume_ref[0] = value
     tiles[me] = (value - 1.0).astype(BF16)

time: 27 us -> 26.5 us (0.981)
  Pallas kernels: 26.2 us -> 25.7 us
    pallas_call x1, Pallas kernels: 25.3 us -> 24.9 us  [on_device(): pl.pallas_call(functools.partial(kernel, n_orient, n_frame), out_shape=(p...]
where the time goes in v5:
time: 26.5 us; the launch traced here: 26.4 us
  Pallas kernels  25.7 us (97%)
  between operations  0.64 us (2%)
    pallas_call x1, Pallas kernels, on_device(): pl.pallas_call(functools.partial(kernel, n_orient, n_frame), out_shape=(p...  24.9 us
    pallas_call x1, Pallas kernels, on_device(): pl.pallas_call(place, out_shape=tuple((jax.ShapeDtypeStruct(value.shape,...  0.83 us

profile of v5, /device:TPU:0, one launch (start us, length us, event | category | flops | bytes accessed | tf_op | source)
XLA Modules:
  0.0 26.4 jit_solution(10818868883158789056)
XLA Ops:
  0.6 24.9 %shard_map.76 = (bf16[128,2048]{1,0:T(8,128)(2,1)S(1)}, f32[1,24,128]{2,1,0:T(8,128)S(1)}, f32[1,256]{1,0:T(1,128)S(1)}) custom-call(bf16[128,4096]{1,0:T(8,128)(2,1)} %logt_hbm.1, s32[256,4096]{1,0:T(8,128)} %frames_hbm.1, s32[2,16,128]{2,1,0:T(8,128)} %index_hbm.1, f32[2,16,128]{2,1,0:T(8,128)} %weight_hbm.1, f32[1,24,128]{2,1,0:T(8,128)} %prior_hbm.1), custom_call_target="tpu_custom_call" | custom-call | tf_op jit(solution)/shard_map/pallas_call | solution.py:576
  25.6 0.8 %shard_map.77 = (bf16[128,2048]{1,0:T(8,128)(2,1)}, f32[1,24,128]{2,1,0:T(8,128)}, f32[1,256]{1,0:T(1,128)}) custom-call(bf16[128,2048]{1,0:T(8,128)(2,1)S(1)} %get-tuple-element.9.a_in, f32[1,24,128]{2,1,0:T(8,128)S(1)} %get-tuple-element.10.b_in, f32[1,256]{1,0:T(1,128)S(1)} %get-tuple-element.11.c_in), custom_call_target="tpu_custom_call" | custom-call | tf_op jit(solution)/shard_map/pallas_call | solution.py:628
